TPU v7x, 32 devices: a whole 2x2x4 slice. The times are simulated.
32 devices in a mesh: grp: 2 (over y), cand: 8 (over z, x), head: 2 (over core).
Axes of the slice: x: 2, y: 2, z: 4, core: 2. Of those that a mesh axis runs over, the one named last changes fastest.
Arguments:
- queries: bfloat16 [8192, 2560], P(('grp', 'cand'), 'head'), parts along dimension 0, may hold values from -130 to 130
- keys: bfloat16 [8192, 512], P(('grp', 'cand'), 'head'), parts along dimension 0, may hold values from -5 to 5
- values: bfloat16 [8192, 512], P(('grp', 'cand'), 'head'), parts along dimension 0, may hold values from -6 to 6
- lengths: int32 [16], P('grp'), parts along dimension 0, may hold values from 257 to 512, as said below
- winners: int32 [8], P('grp'), parts along dimension 0, may hold values from 0 to 1
- score_weight: float32 [2560], P('head'), may hold values from -16 to 16
Outputs:
- first_round: bfloat16 [8192, 2560], P(('grp', 'cand'), 'head'), parts along dimension 0
- second_round: bfloat16 [4096, 2560], P(('grp', 'cand'), 'head'), parts along dimension 0
- first_score: float32 [16], P(('grp', 'cand')), parts along dimension 0
- final_round_score: float32 [16], P(('grp', 'cand')), parts along dimension 0
There are 2 independent parts, one for each index of `grp`. A program takes and returns all parts, laid end to end along the dimension named above; an argument that names none is the same for every part. Nothing has to cross between parts.
Inputs may be any that keep to these rules, and one draw needn't show every extreme that they name: lengths of all candidates lie in this range; some candidate uses all 512 slots. `winners`: 0 picks the even member 2 j of pair j, 1 the odd one.
All inputs are finite; a program needn't handle non-finite values.
Results may differ from a plain program's by a relative error of at most 0.0049.
Values may be sent and summed in bfloat16 or wider, within the bound.
A program may use at most 128 MiB of HBM per device.

v0:
```python
import functools

import jax
import jax.numpy as jnp
from jax import lax
from jax.experimental import pallas as pl
from jax.experimental.pallas import tpu as pltpu
from jax.sharding import PartitionSpec as P

HD = 128
LOG2E = 1.4426950408889634
MESH = pl.DeviceIdType.MESH
NEG = -1e30
PAD = 16
OUT = pltpu.VMEM


def kernel(
    heads, groups, span,
    q_hbm, k_hbm, v_hbm, len_hbm, win_hbm, w_hbm,
    o_1, o_2, judged_ref,
    q_v, k_o, v_o, k_x, v_x, q_x, k_s, k_c, v_s, v_c, vt, bias,
    acc, top, len_ref, win_ref, w_ref, part_1, part_2, got_1, got_2,
    load_sem, xs, xr, zs, zr, qs, qr, small_sem, ps, pr,
):
    half = span // 2
    ratio = heads // groups
    me = lax.axis_index("cand")
    bit = lax.rem(me, 2)
    hd = lax.axis_index("head")
    pair = me // 2
    mate = me + 1 - 2 * bit
    pair_bit = lax.rem(pair, 2)
    rival_pair = pair + 1 - 2 * pair_bit
    across = 2 * rival_pair + bit
    other = 1 - hd

    barrier = pltpu.get_barrier_semaphore()
    peers = [
        {"cand": mate}, {"cand": across}, {"head": other}, {"cand": mate, "head": other},
    ]
    for peer in peers:
        pl.semaphore_signal(barrier, inc=1, device_id=peer, device_id_type=MESH)

    def col(i):
        return pl.ds(pl.multiple_of(i * HD, HD), HD)

    loads = []
    for g in range(groups):
        loads.append(pltpu.make_async_copy(k_hbm.at[:, col(g)], k_o.at[g], load_sem.at[2 * g]))
        loads.append(pltpu.make_async_copy(v_hbm.at[:, col(g)], v_o.at[g], load_sem.at[2 * g + 1]))
    for h in range(heads):
        loads.append(
            pltpu.make_async_copy(q_hbm.at[:, col(h)], q_v.at[h], load_sem.at[2 * groups + h])
        )
    small = [
        pltpu.make_async_copy(src, dst, small_sem.at[i])
        for i, (src, dst) in enumerate(((len_hbm, len_ref), (win_hbm, win_ref), (w_hbm, w_ref)))
    ]
    for c in small:
        c.start()
    pl.semaphore_wait(barrier, len(peers))

    def remote(src, dst, s, r, peer):
        return pltpu.make_async_remote_copy(
            src_ref=src, dst_ref=dst, send_sem=s, recv_sem=r,
            device_id=peer, device_id_type=MESH,
        )

    x_copies, f_copies = [], []
    for g in range(groups):
        for j, (src, dst, fsrc, fdst) in enumerate(
            ((k_hbm, k_x, k_s, k_c), (v_hbm, v_x, v_s, v_c))
        ):
            i = 2 * g + j
            x_copies.append(
                remote(src.at[:, col(g)], dst.at[g], xs.at[i], xr.at[i], {"cand": mate})
            )
            f_copies.append(remote(fsrc.at[g], fdst.at[g], zs.at[i], zr.at[i], {"cand": across}))
    sent = pl.ds(pl.multiple_of((1 - bit) * half, half), half)
    mine = pl.ds(pl.multiple_of(bit * half, half), half)

    def q_copy(h):
        return remote(q_hbm.at[sent, col(h)], q_x.at[h], qs.at[h], qr.at[h], {"cand": mate})

    for c in x_copies:
        c.start()
    for c in loads:
        c.start()
    for h in range(heads):
        q_copy(h).start()
    for c in small:
        c.wait()

    won = win_ref[pair]
    i_won = won == bit
    rival_won = win_ref[rival_pair]
    len_me = len_ref[me]
    len_mate = len_ref[mate]
    len_s = len_ref[2 * pair + won]
    len_c = len_ref[2 * rival_pair + rival_won]
    scale = HD ** (-0.5) * LOG2E
    tail = lax.broadcasted_iota(jnp.int32, (half, HD), 0) + half
    for i, n in enumerate((len_me, len_mate, len_s, len_c)):
        bias[i] = jnp.where(tail < n, 0.0, NEG).astype(jnp.float32)
        for g in range(groups):
            vt[i, g, HD:, :] = jnp.ones((PAD, span), jnp.bfloat16)

    def scores(k, q):
        return lax.dot_general(k, q, (((1,), (1,)), ((), ())), preferred_element_type=jnp.float32)

    def masked(s, i):
        b = bias[i]
        return s[:half], s[half:] + jnp.concatenate([b] * (s.shape[1] // HD), axis=1)

    def key_max(parts):
        peak = parts[0]
        for s in parts[1:]:
            peak = jnp.maximum(peak, s)
        return jnp.max(peak, axis=0, keepdims=True)

    def weighted(parts, peak, v):
        p = jnp.concatenate([jnp.exp2((s - peak) * scale).astype(jnp.bfloat16) for s in parts], axis=0)
        return jnp.dot(v, p, preferred_element_type=jnp.float32)

    def finish(o, first_row, n):
        rows = lax.broadcasted_iota(jnp.int32, (1, o.shape[1]), 1) + first_row
        inverse = jnp.where(rows < n, 1.0 / o[HD : HD + 1], 0.0)
        return jnp.transpose(o[:HD] * inverse).astype(jnp.bfloat16)

    def judged(out, h):
        x = jnp.sum(out.astype(jnp.float32).reshape(-1, 8, HD), axis=0)
        return x * w_ref[h * HD : (h + 1) * HD].reshape(1, HD)

    def pipeline(items, first, rest):
        ahead = first(*items[0])
        for i, item in enumerate(items):
            now = ahead
            if i + 1 < len(items):
                ahead = first(*items[i + 1])
            rest(now, *item)

    def group_blocks(g):
        return [(h, c) for h in range(g * ratio, (g + 1) * ratio) for c in range(0, span, half)]

    for c in loads[: 2 * groups]:
        c.wait()
    for g in range(groups):
        vt[0, g, :HD, :] = jnp.transpose(v_o[g])

    def own_scores(h, c):
        if c == 0:
            loads[2 * groups + h].wait()
        return scores(k_o[h // ratio], q_v[h, c : c + half])

    def own_rest(s, h, c):
        parts = masked(s, 0)
        peak = key_max(parts)
        acc[h, :, c : c + half] = weighted(parts, peak, vt[0, h // ratio])
        top[h, :, c : c + half] = jnp.broadcast_to(peak, (8, half))

    pipeline([b for g in range(groups) for b in group_blocks(g)], own_scores, own_rest)

    sums = {1: jnp.zeros((8, HD), jnp.float32), 2: jnp.zeros((8, HD), jnp.float32)}

    def mate_scores(h, c):
        return scores(k_x[h // ratio], q_v[h, c : c + half])

    def mate_rest(s, h, c):
        parts = masked(s, 1)
        before = top[h, :1, c : c + half]
        peak = jnp.maximum(before, key_max(parts))
        keep = jnp.exp2((before - peak) * scale)
        o = weighted(parts, peak, vt[1, h // ratio]) + acc[h, :, c : c + half] * keep
        out = finish(o, c, len_me)
        o_1[h, c : c + half] = out
        sums[1] += judged(out, h)

    for g in range(groups):
        for j in range(2):
            x_copies[2 * g + j].wait_recv()
        k_s[g] = jnp.where(i_won, k_o[g], k_x[g])
        v_s[g] = jnp.where(i_won, v_o[g], v_x[g])
        vt[1, g, :HD, :] = jnp.transpose(v_x[g])
        for j in range(2):
            f_copies[2 * g + j].start()
        pipeline(group_blocks(g), mate_scores, mate_rest)
    part_1[...] = sums[1]


    def second_scores(h):
        g = h // ratio
        q_copy(h).wait_recv()
        q = jnp.where(i_won, q_v[h, mine, :], q_x[h])
        return scores(k_s[g], q), scores(k_c[g], q)

    def second_rest(s, h):
        g = h // ratio
        a, b = masked(s[0], 2), masked(s[1], 3)
        peak = key_max(a + b)
        o = weighted(a, peak, vt[2, g]) + weighted(b, peak, vt[3, g])
        out = finish(o, bit * half, len_s)
        o_2[h] = out
        sums[2] += judged(out, h)

    send_1 = remote(part_1, got_1, ps.at[0], pr.at[0], {"head": other})
    for g in range(groups):
        vt[2, g, :HD, :] = jnp.where(i_won, vt[0, g, :HD, :], vt[1, g, :HD, :])
        for j in range(2):
            f_copies[2 * g + j].wait_recv()
        vt[3, g, :HD, :] = jnp.transpose(v_c[g])
        if g == 0:
            send_1.start()
        pipeline([(h,) for h in range(g * ratio, (g + 1) * ratio)], second_scores, second_rest)
    part_2[...] = sums[2]

    def over(x, n):
        return x / jnp.full((8, HD), n.astype(jnp.float32))

    send_1.wait()
    judged_ref[0] = over(part_1[...] + got_1[...], len_me)
    sends = [
        remote(part_2, got_2.at[i], ps.at[1 + i], pr.at[1 + i], peer)
        for i, peer in enumerate(({"head": other}, {"cand": mate}, {"cand": mate, "head": other}))
    ]
    for c in sends:
        c.start()
    for c in x_copies + f_copies:
        c.wait_send()
    for h in range(heads):
        q_copy(h).wait_send()
    for c in sends:
        c.wait()
    judged_ref[1] = over((part_2[...] + got_2[0]) + (got_2[1] + got_2[2]), len_s)


def put_out(heads, o_1, o_2, judged_ref, first_hbm, second_hbm, s1_ref, s2_ref, sem):
    copies = []
    for h in range(heads):
        cols = pl.ds(h * HD, HD)
        copies.append(pltpu.make_async_copy(o_1.at[h], first_hbm.at[:, cols], sem.at[h]))
        copies.append(pltpu.make_async_copy(o_2.at[h], second_hbm.at[:, cols], sem.at[heads + h]))
    for c in copies:
        c.start()
    s1_ref[0] = jnp.sum(judged_ref[0])
    s2_ref[0] = jnp.sum(judged_ref[1])
    for c in copies:
        c.wait()


def body(queries, keys, values, lengths, winners, score_weight):
    span = queries.shape[0]
    half = span // 2
    heads = queries.shape[1] // HD
    groups = keys.shape[1] // HD
    bf16, f32 = jnp.bfloat16, jnp.float32
    hbm = pl.BlockSpec(memory_space=pl.ANY)
    smem = pl.BlockSpec(memory_space=pltpu.SMEM)
    vmem = pl.BlockSpec(memory_space=pltpu.VMEM)
    dma = pltpu.SemaphoreType.DMA
    kv = pltpu.VMEM((groups, span, HD), bf16)
    o_1, o_2, judged = pl.pallas_call(
        functools.partial(kernel, heads, groups, span),
        out_shape=(
            OUT((heads, span, HD), bf16),
            OUT((heads, half, HD), bf16),
            OUT((2, 8, HD), f32),
        ),
        in_specs=[hbm] * 6,
        out_specs=(vmem,) * 3,
        scratch_shapes=[
            pltpu.VMEM((heads, span, HD), bf16),
            kv, kv, kv, kv,
            pltpu.VMEM((heads, half, HD), bf16),
            kv, kv, kv, kv,
            pltpu.VMEM((4, groups, HD + PAD, span), bf16),
            pltpu.VMEM((4, half, HD), f32),
            pltpu.VMEM((heads, HD + PAD, span), f32),
            pltpu.VMEM((heads, 8, span), f32),
            pltpu.SMEM(lengths.shape, jnp.int32),
            pltpu.SMEM(winners.shape, jnp.int32),
            pltpu.VMEM(score_weight.shape, f32),
            pltpu.VMEM((8, HD), f32),
            pltpu.VMEM((8, HD), f32),
            pltpu.VMEM((8, HD), f32),
            pltpu.VMEM((3, 8, HD), f32),
            dma((2 * groups + heads,)),
            dma((2 * groups,)), dma((2 * groups,)),
            dma((2 * groups,)), dma((2 * groups,)),
            dma((heads,)), dma((heads,)),
            dma((3,)),
            dma((4,)), dma((4,)),
        ],
        compiler_params=pltpu.CompilerParams(collective_id=0, has_side_effects=True),
    )(queries, keys, values, lengths, winners, score_weight)
    return pl.pallas_call(
        functools.partial(put_out, heads),
        out_shape=(
            jax.ShapeDtypeStruct(queries.shape, bf16),
            jax.ShapeDtypeStruct((half, queries.shape[1]), bf16),
            jax.ShapeDtypeStruct((1,), f32),
            jax.ShapeDtypeStruct((1,), f32),
        ),
        in_specs=[vmem] * 3,
        out_specs=(hbm, hbm, smem, smem),
        scratch_shapes=[dma((2 * heads,))],
        compiler_params=pltpu.CompilerParams(vmem_limit_bytes=1 << 20),
    )(*(pltpu.with_memory_space_constraint(x, pltpu.VMEM) for x in (o_1, o_2, judged)))


def solution(mesh):
    in_specs = (
        P(("grp", "cand"), "head"),
        P(("grp", "cand"), "head"),
        P(("grp", "cand"), "head"),
        P("grp"),
        P("grp"),
        P("head"),
    )
    out_specs = (
        P(("grp", "cand"), "head"),
        P(("grp", "cand"), "head"),
        P(("grp", "cand")),
        P(("grp", "cand")),
    )
    return jax.shard_map(body, mesh=mesh, in_specs=in_specs, out_specs=out_specs, check_vma=False)
```

profile of v0, /device:TPU:0, one launch (start us, length us, event | category | flops | bytes accessed | tf_op | source)
XLA Modules:
  0.0 37.2 jit_solution(2054145432426390615)
XLA Ops:
  0.6 34.5 %shard_map.93 = (bf16[10,512,128]{2,1,0:T(8,128)(2,1)S(1)}, bf16[10,256,128]{2,1,0:T(8,128)(2,1)S(1)}, f32[2,8,128]{2,1,0:T(8,128)S(1)}) custom-call(bf16[512,1280]{1,0:T(8,128)(2,1)} %q_hbm.1, bf16[512,256]{1,0:T(8,128)(2,1)} %k_hbm.1, bf16[512,256]{1,0:T(8,128)(2,1)} %v_hbm.1, s32[8]{0:T(128)} %len_hbm.1, s32[4]{0:T(128)} %win_hbm.1, f32[1280]{0:T(1024)} %w_hbm.1), custom_call_target="tpu_custom_call" | custom-call | tf_op jit(solution)/shard_map/pallas_call | solution.py:262
  35.1 2.0 %shard_map.94 = (bf16[512,1280]{1,0:T(8,128)(2,1)}, bf16[256,1280]{1,0:T(8,128)(2,1)}, f32[1]{0:T(128)}, f32[1]{0:T(128)}) custom-call(bf16[10,512,128]{2,1,0:T(8,128)(2,1)S(1)} %get-tuple-element.7.o_1, bf16[10,256,128]{2,1,0:T(8,128)(2,1)S(1)} %get-tuple-element.8.o_2, f32[2,8,128]{2,1,0:T(8,128)S(1)} %get-tuple-element.9.judged_ref), custom_call_target="tpu_custom_call" | custom-call | tf_op jit(solution)/shard_map/pallas_call | solution.py:296
where the time goes:
time: 37.4 us; the launch traced here: 37.2 us
  Pallas kernels  36.4 us (97%)
  between operations  0.8 us (2%)
    pallas_call x1, Pallas kernels, body(): pl.pallas_call(functools.partial(kernel, heads, groups, span), out_shape=...  34.5 us
    pallas_call x1, Pallas kernels, body(): pl.pallas_call(functools.partial(put_out, heads), out_shape=(jax.ShapeDty...  1.95 us

commit v1 on v0

--- a/solution.py
+++ b/solution.py
@@ -20,8 +20,8 @@
     q_hbm, k_hbm, v_hbm, len_hbm, win_hbm, w_hbm,
     o_1, o_2, judged_ref,
     q_v, k_o, v_o, k_x, v_x, q_x, k_s, k_c, v_s, v_c, vt, bias,
-    acc, top, len_ref, win_ref, w_ref, part_1, part_2, got_1, got_2,
-    load_sem, xs, xr, zs, zr, qs, qr, small_sem, ps, pr,
+    acc, top, len_ref, win_ref, w_ref, part_1, part_2, part_3, got_1, got_2, got_3,
+    load_sem, xs, xr, zs, zr, qs, qr, small_sem, ps, pr, z_in, core_in,
 ):
     half = span // 2
     ratio = heads // groups
@@ -36,11 +36,11 @@
     other = 1 - hd
 
     barrier = pltpu.get_barrier_semaphore()
-    peers = [
-        {"cand": mate}, {"cand": across}, {"head": other}, {"cand": mate, "head": other},
-    ]
-    for peer in peers:
-        pl.semaphore_signal(barrier, inc=1, device_id=peer, device_id_type=MESH)
+    pl.semaphore_signal(barrier, inc=1, device_id={"cand": mate}, device_id_type=MESH)
+    pl.semaphore_signal(
+        barrier, inc=1, device_id={"cand": jnp.where(hd == 0, me, across), "head": 1},
+        device_id_type=MESH,
+    )
 
     def col(i):
         return pl.ds(pl.multiple_of(i * HD, HD), HD)
@@ -57,9 +57,7 @@
         pltpu.make_async_copy(src, dst, small_sem.at[i])
         for i, (src, dst) in enumerate(((len_hbm, len_ref), (win_hbm, win_ref), (w_hbm, w_ref)))
     ]
-    for c in small:
-        c.start()
-    pl.semaphore_wait(barrier, len(peers))
+    pl.semaphore_wait(barrier, 1 + 2 * hd)
 
     def remote(src, dst, s, r, peer):
         return pltpu.make_async_remote_copy(
@@ -77,20 +75,29 @@
                 remote(src.at[:, col(g)], dst.at[g], xs.at[i], xr.at[i], {"cand": mate})
             )
             f_copies.append(remote(fsrc.at[g], fdst.at[g], zs.at[i], zr.at[i], {"cand": across}))
-    sent = pl.ds(pl.multiple_of((1 - bit) * half, half), half)
-    mine = pl.ds(pl.multiple_of(bit * half, half), half)
-
-    def q_copy(h):
-        return remote(q_hbm.at[sent, col(h)], q_x.at[h], qs.at[h], qr.at[h], {"cand": mate})
+
+    quarter = half // 2
+    chunks = [(h, 0, half) for h in range(heads - 1)]
+    chunks += [(heads - 1, r, quarter) for r in (0, quarter)]
+    q_copies = []
+    for i, (h, r, n) in enumerate(chunks):
+        rows = pl.ds(pl.multiple_of((1 - bit) * half + r, quarter), n)
+        q_copies.append(
+            remote(q_hbm.at[rows, col(h)], q_x.at[h, r : r + n], qs.at[i], qr.at[i], {"cand": mate})
+        )
 
     for c in x_copies:
         c.start()
-    for c in loads:
+    for c in small + loads:
         c.start()
-    for h in range(heads):
-        q_copy(h).start()
+    for c in q_copies:
+        c.start()
     for c in small:
         c.wait()
+
+    @pl.when(hd == 1)
+    def _():
+        pl.semaphore_signal(z_in.at[0], inc=1, device_id={"cand": across}, device_id_type=MESH)
 
     won = win_ref[pair]
     i_won = won == bit
@@ -161,7 +168,16 @@
 
     pipeline([b for g in range(groups) for b in group_blocks(g)], own_scores, own_rest)
 
-    sums = {1: jnp.zeros((8, HD), jnp.float32), 2: jnp.zeros((8, HD), jnp.float32)}
+    @pl.when(hd == 1)
+    def _():
+        pl.semaphore_wait(z_in.at[0], 1)
+        pl.semaphore_signal(core_in.at[0], inc=1, device_id={"head": 0}, device_id_type=MESH)
+
+    @pl.when(hd == 0)
+    def _():
+        pl.semaphore_wait(core_in.at[0], 1)
+
+    sums = {i: jnp.zeros((8, HD), jnp.float32) for i in (1, 2, 3)}
 
     def mate_scores(h, c):
         return scores(k_x[h // ratio], q_v[h, c : c + half])
@@ -188,22 +204,43 @@
     part_1[...] = sums[1]
 
 
-    def second_scores(h):
+    def second_scores(i):
+        h, r, n = chunks[i]
         g = h // ratio
-        q_copy(h).wait_recv()
-        q = jnp.where(i_won, q_v[h, mine, :], q_x[h])
+        q_copies[i].wait_recv()
+        rows = pl.ds(pl.multiple_of(bit * half + r, quarter), n)
+        q = jnp.where(i_won, q_v[h, rows, :], q_x[h, r : r + n])
         return scores(k_s[g], q), scores(k_c[g], q)
 
-    def second_rest(s, h):
+    def second_rest(s, i):
+        h, r, n = chunks[i]
         g = h // ratio
         a, b = masked(s[0], 2), masked(s[1], 3)
         peak = key_max(a + b)
         o = weighted(a, peak, vt[2, g]) + weighted(b, peak, vt[3, g])
-        out = finish(o, bit * half, len_s)
-        o_2[h] = out
-        sums[2] += judged(out, h)
-
+        out = finish(o, bit * half + r, len_s)
+        o_2[h, r : r + n] = out
+        if h < early:
+            sums[2] += judged(out, h)
+
+    def ahead_scores(h, c):
+        return scores(k_c[h // ratio], q_v[h, c : c + half])
+
+    def ahead_rest(s, h, c):
+        parts = masked(s, 3)
+        before = top[h, :1, c : c + half]
+        peak = jnp.maximum(before, key_max(parts))
+        keep = jnp.exp2((before - peak) * scale)
+        o = weighted(parts, peak, vt[3, h // ratio]) + acc[h, :, c : c + half] * keep
+        sums[3] += judged(finish(o, c, len_me), h)
+
+    def over(x, n):
+        return x / jnp.full((8, HD), n.astype(jnp.float32))
+
+    early = heads - min(3, ratio)
     send_1 = remote(part_1, got_1, ps.at[0], pr.at[0], {"head": other})
+    send_2 = remote(part_2, got_2, ps.at[1], pr.at[1], {"head": other})
+    send_3 = remote(part_3, got_3, ps.at[2], pr.at[2], {"cand": mate})
     for g in range(groups):
         vt[2, g, :HD, :] = jnp.where(i_won, vt[0, g, :HD, :], vt[1, g, :HD, :])
         for j in range(2):
@@ -211,30 +248,32 @@
         vt[3, g, :HD, :] = jnp.transpose(v_c[g])
         if g == 0:
             send_1.start()
-        pipeline([(h,) for h in range(g * ratio, (g + 1) * ratio)], second_scores, second_rest)
-    part_2[...] = sums[2]
-
-    def over(x, n):
-        return x / jnp.full((8, HD), n.astype(jnp.float32))
-
+        pipeline(
+            [(i,) for i, (h, _, _) in enumerate(chunks) if h // ratio == g and h < early],
+            second_scores, second_rest,
+        )
+    pipeline(
+        [(h, c) for h in range(early, heads) for c in range(0, span, half)],
+        ahead_scores, ahead_rest,
+    )
+    part_2[...] = sums[2] + jnp.where(i_won, sums[3], 0.0)
+    late = [(i,) for i, (h, _, _) in enumerate(chunks) if h >= early]
+    pipeline(late[:1], second_scores, second_rest)
+    send_2.start()
     send_1.wait()
     judged_ref[0] = over(part_1[...] + got_1[...], len_me)
-    sends = [
-        remote(part_2, got_2.at[i], ps.at[1 + i], pr.at[1 + i], peer)
-        for i, peer in enumerate(({"head": other}, {"cand": mate}, {"cand": mate, "head": other}))
-    ]
-    for c in sends:
-        c.start()
-    for c in x_copies + f_copies:
+    pipeline(late[1:2], second_scores, second_rest)
+    send_2.wait()
+    part_3[...] = part_2[...] + got_2[...]
+    send_3.start()
+    pipeline(late[2:], second_scores, second_rest)
+    for c in x_copies + f_copies + q_copies:
         c.wait_send()
-    for h in range(heads):
-        q_copy(h).wait_send()
-    for c in sends:
-        c.wait()
-    judged_ref[1] = over((part_2[...] + got_2[0]) + (got_2[1] + got_2[2]), len_s)
-
-
-def put_out(heads, o_1, o_2, judged_ref, first_hbm, second_hbm, s1_ref, s2_ref, sem):
+    send_3.wait()
+    judged_ref[1] = over(part_3[...] + got_3[...], len_s)
+
+
+def put_out(heads, o_1, o_2, judged_ref, first_hbm, second_hbm, s1_hbm, s2_hbm, s1, s2, sem):
     copies = []
     for h in range(heads):
         cols = pl.ds(h * HD, HD)
@@ -242,8 +281,10 @@
         copies.append(pltpu.make_async_copy(o_2.at[h], second_hbm.at[:, cols], sem.at[heads + h]))
     for c in copies:
         c.start()
-    s1_ref[0] = jnp.sum(judged_ref[0])
-    s2_ref[0] = jnp.sum(judged_ref[1])
+    for i, (s, dst) in enumerate(((s1, s1_hbm), (s2, s2_hbm))):
+        s[0] = jnp.sum(judged_ref[i])
+        copies.append(pltpu.make_async_copy(s, dst, sem.at[2 * heads + i]))
+        copies[-1].start()
     for c in copies:
         c.wait()
 
@@ -255,7 +296,6 @@
     groups = keys.shape[1] // HD
     bf16, f32 = jnp.bfloat16, jnp.float32
     hbm = pl.BlockSpec(memory_space=pl.ANY)
-    smem = pl.BlockSpec(memory_space=pltpu.SMEM)
     vmem = pl.BlockSpec(memory_space=pltpu.VMEM)
     dma = pltpu.SemaphoreType.DMA
     kv = pltpu.VMEM((groups, span, HD), bf16)
@@ -280,16 +320,14 @@
             pltpu.SMEM(lengths.shape, jnp.int32),
             pltpu.SMEM(winners.shape, jnp.int32),
             pltpu.VMEM(score_weight.shape, f32),
-            pltpu.VMEM((8, HD), f32),
-            pltpu.VMEM((8, HD), f32),
-            pltpu.VMEM((8, HD), f32),
-            pltpu.VMEM((3, 8, HD), f32),
+            *[pltpu.VMEM((8, HD), f32)] * 6,
             dma((2 * groups + heads,)),
             dma((2 * groups,)), dma((2 * groups,)),
             dma((2 * groups,)), dma((2 * groups,)),
-            dma((heads,)), dma((heads,)),
+            dma((heads + 1,)), dma((heads + 1,)),
             dma((3,)),
-            dma((4,)), dma((4,)),
+            dma((3,)), dma((3,)),
+            pltpu.SemaphoreType.REGULAR((1,)), pltpu.SemaphoreType.REGULAR((1,)),
         ],
         compiler_params=pltpu.CompilerParams(collective_id=0, has_side_effects=True),
     )(queries, keys, values, lengths, winners, score_weight)
@@ -302,8 +340,8 @@
             jax.ShapeDtypeStruct((1,), f32),
         ),
         in_specs=[vmem] * 3,
-        out_specs=(hbm, hbm, smem, smem),
-        scratch_shapes=[dma((2 * heads,))],
+        out_specs=(hbm,) * 4,
+        scratch_shapes=[pltpu.SMEM((1,), f32)] * 2 + [dma((2 * heads + 2,))],
         compiler_params=pltpu.CompilerParams(vmem_limit_bytes=1 << 20),
     )(*(pltpu.with_memory_space_constraint(x, pltpu.VMEM) for x in (o_1, o_2, judged)))
 

time: 37.4 us -> 36.1 us (0.965)
  Pallas kernels: 36.4 us -> 35.2 us
    pallas_call x1, Pallas kernels: 34.5 us -> 33.7 us  [body(): pl.pallas_call(functools.partial(kernel, heads, groups, span), out_shape=...]
    pallas_call x1, Pallas kernels: 1.95 us -> 1.46 us  [body(): pl.pallas_call(functools.partial(put_out, heads), out_shape=(jax.ShapeDty...]
where the time goes in v1:
time: 36.1 us; the launch traced here: 36 us
  Pallas kernels  35.2 us (98%)
  between operations  0.8 us (2%)
    pallas_call x1, Pallas kernels, body(): pl.pallas_call(functools.partial(kernel, heads, groups, span), out_shape=...  33.7 us
    pallas_call x1, Pallas kernels, body(): pl.pallas_call(functools.partial(put_out, heads), out_shape=(jax.ShapeDty...  1.46 us

profile of v1, /device:TPU:0, one launch (start us, length us, event | category | flops | bytes accessed | tf_op | source)
XLA Modules:
  0.0 36.0 jit_solution(8490570792521099015)
XLA Ops:
  0.6 33.7 %shard_map.93 = (bf16[10,512,128]{2,1,0:T(8,128)(2,1)S(1)}, bf16[10,256,128]{2,1,0:T(8,128)(2,1)S(1)}, f32[2,8,128]{2,1,0:T(8,128)S(1)}) custom-call(bf16[512,1280]{1,0:T(8,128)(2,1)} %q_hbm.1, bf16[512,256]{1,0:T(8,128)(2,1)} %k_hbm.1, bf16[512,256]{1,0:T(8,128)(2,1)} %v_hbm.1, s32[8]{0:T(128)} %len_hbm.1, s32[4]{0:T(128)} %win_hbm.1, f32[1280]{0:T(1024)} %w_hbm.1), custom_call_target="tpu_custom_call" | custom-call | tf_op jit(solution)/shard_map/pallas_call | solution.py:302
  34.4 1.5 %shard_map.94 = (bf16[512,1280]{1,0:T(8,128)(2,1)}, bf16[256,1280]{1,0:T(8,128)(2,1)}, f32[1]{0:T(128)}, f32[1]{0:T(128)}) custom-call(bf16[10,512,128]{2,1,0:T(8,128)(2,1)S(1)} %get-tuple-element.7.o_1, bf16[10,256,128]{2,1,0:T(8,128)(2,1)S(1)} %get-tuple-element.8.o_2, f32[2,8,128]{2,1,0:T(8,128)S(1)} %get-tuple-element.9.judged_ref), custom_call_target="tpu_custom_call" | custom-call | tf_op jit(solution)/shard_map/pallas_call | solution.py:334

commit v2 on v1

--- a/solution.py
+++ b/solution.py
@@ -92,12 +92,15 @@
         c.start()
     for c in q_copies:
         c.start()
-    for c in small:
-        c.wait()
 
     @pl.when(hd == 1)
     def _():
         pl.semaphore_signal(z_in.at[0], inc=1, device_id={"cand": across}, device_id_type=MESH)
+        pl.semaphore_wait(z_in.at[0], 1)
+        pl.semaphore_signal(core_in.at[0], inc=1, device_id={"head": 0}, device_id_type=MESH)
+
+    for c in small:
+        c.wait()
 
     won = win_ref[pair]
     i_won = won == bit
@@ -166,16 +169,25 @@
         acc[h, :, c : c + half] = weighted(parts, peak, vt[0, h // ratio])
         top[h, :, c : c + half] = jnp.broadcast_to(peak, (8, half))
 
-    pipeline([b for g in range(groups) for b in group_blocks(g)], own_scores, own_rest)
-
-    @pl.when(hd == 1)
-    def _():
-        pl.semaphore_wait(z_in.at[0], 1)
-        pl.semaphore_signal(core_in.at[0], inc=1, device_id={"head": 0}, device_id_type=MESH)
+    def forward_k(g):
+        x_copies[2 * g].wait_recv()
+        k_s[g] = jnp.where(i_won, k_o[g], k_x[g])
+        f_copies[2 * g].start()
+
+    def forward_v(g):
+        x_copies[2 * g + 1].wait_recv()
+        v_s[g] = jnp.where(i_won, v_o[g], v_x[g])
+        f_copies[2 * g + 1].start()
+        vt[1, g, :HD, :] = jnp.transpose(v_x[g])
+
+    pipeline(group_blocks(0), own_scores, own_rest)
 
     @pl.when(hd == 0)
     def _():
         pl.semaphore_wait(core_in.at[0], 1)
+
+    forward_k(0)
+    pipeline([b for g in range(1, groups) for b in group_blocks(g)], own_scores, own_rest)
 
     sums = {i: jnp.zeros((8, HD), jnp.float32) for i in (1, 2, 3)}
 
@@ -193,16 +205,11 @@
         sums[1] += judged(out, h)
 
     for g in range(groups):
-        for j in range(2):
-            x_copies[2 * g + j].wait_recv()
-        k_s[g] = jnp.where(i_won, k_o[g], k_x[g])
-        v_s[g] = jnp.where(i_won, v_o[g], v_x[g])
-        vt[1, g, :HD, :] = jnp.transpose(v_x[g])
-        for j in range(2):
-            f_copies[2 * g + j].start()
+        if g:
+            forward_k(g)
+        forward_v(g)
         pipeline(group_blocks(g), mate_scores, mate_rest)
     part_1[...] = sums[1]
-
 
     def second_scores(i):
         h, r, n = chunks[i]
@@ -237,36 +244,42 @@
     def over(x, n):
         return x / jnp.full((8, HD), n.astype(jnp.float32))
 
-    early = heads - min(3, ratio)
+    early = heads - ratio
     send_1 = remote(part_1, got_1, ps.at[0], pr.at[0], {"head": other})
     send_2 = remote(part_2, got_2, ps.at[1], pr.at[1], {"head": other})
     send_3 = remote(part_3, got_3, ps.at[2], pr.at[2], {"cand": mate})
-    for g in range(groups):
+
+    def challenger(g):
         vt[2, g, :HD, :] = jnp.where(i_won, vt[0, g, :HD, :], vt[1, g, :HD, :])
         for j in range(2):
             f_copies[2 * g + j].wait_recv()
         vt[3, g, :HD, :] = jnp.transpose(v_c[g])
-        if g == 0:
-            send_1.start()
-        pipeline(
-            [(i,) for i, (h, _, _) in enumerate(chunks) if h // ratio == g and h < early],
-            second_scores, second_rest,
-        )
+
+    def second(first, end):
+        for i in range(first, end):
+            second_rest(second_scores(i), i)
+
+    ahead = early // 2 + 1
+    challenger(0)
+    send_1.start()
+    second(0, ahead)
+    for g in range(1, groups):
+        challenger(g)
     pipeline(
         [(h, c) for h in range(early, heads) for c in range(0, span, half)],
         ahead_scores, ahead_rest,
     )
+    second(ahead, early)
     part_2[...] = sums[2] + jnp.where(i_won, sums[3], 0.0)
-    late = [(i,) for i, (h, _, _) in enumerate(chunks) if h >= early]
-    pipeline(late[:1], second_scores, second_rest)
-    send_2.start()
     send_1.wait()
     judged_ref[0] = over(part_1[...] + got_1[...], len_me)
-    pipeline(late[1:2], second_scores, second_rest)
+    send_2.start()
+    second(early, early + 2)
     send_2.wait()
     part_3[...] = part_2[...] + got_2[...]
+    second(early + 2, early + 3)
     send_3.start()
-    pipeline(late[2:], second_scores, second_rest)
+    second(early + 3, len(chunks))
     for c in x_copies + f_copies + q_copies:
         c.wait_send()
     send_3.wait()

time: 36.1 us -> 34.6 us (0.958)
  Pallas kernels: 35.2 us -> 33.6 us
    pallas_call x1, Pallas kernels: 33.7 us -> 32.2 us  [body(): pl.pallas_call(functools.partial(kernel, heads, groups, span), out_shape=...]
where the time goes in v2:
time: 34.6 us; the launch traced here: 34.5 us
  Pallas kernels  33.6 us (97%)
  between operations  0.82 us (2%)
    pallas_call x1, Pallas kernels, body(): pl.pallas_call(functools.partial(kernel, heads, groups, span), out_shape=...  32.2 us
    pallas_call x1, Pallas kernels, body(): pl.pallas_call(functools.partial(put_out, heads), out_shape=(jax.ShapeDty...  1.46 us

profile of v2, /device:TPU:0, one launch (start us, length us, event | category | flops | bytes accessed | tf_op | source)
XLA Modules:
  0.0 34.5 jit_solution(14761442265675284656)
XLA Ops:
  0.6 32.2 %shard_map.93 = (bf16[10,512,128]{2,1,0:T(8,128)(2,1)S(1)}, bf16[10,256,128]{2,1,0:T(8,128)(2,1)S(1)}, f32[2,8,128]{2,1,0:T(8,128)S(1)}) custom-call(bf16[512,1280]{1,0:T(8,128)(2,1)} %q_hbm.1, bf16[512,256]{1,0:T(8,128)(2,1)} %k_hbm.1, bf16[512,256]{1,0:T(8,128)(2,1)} %v_hbm.1, s32[8]{0:T(128)} %len_hbm.1, s32[4]{0:T(128)} %win_hbm.1, f32[1280]{0:T(1024)} %w_hbm.1), custom_call_target="tpu_custom_call" | custom-call | tf_op jit(solution)/shard_map/pallas_call | solution.py:315
  32.8 1.5 %shard_map.94 = (bf16[512,1280]{1,0:T(8,128)(2,1)}, bf16[256,1280]{1,0:T(8,128)(2,1)}, f32[1]{0:T(128)}, f32[1]{0:T(128)}) custom-call(bf16[10,512,128]{2,1,0:T(8,128)(2,1)S(1)} %get-tuple-element.7.o_1, bf16[10,256,128]{2,1,0:T(8,128)(2,1)S(1)} %get-tuple-element.8.o_2, f32[2,8,128]{2,1,0:T(8,128)S(1)} %get-tuple-element.9.judged_ref), custom_call_target="tpu_custom_call" | custom-call | tf_op jit(solution)/shard_map/pallas_call | solution.py:347

commit v3 on v2

--- a/solution.py
+++ b/solution.py
@@ -11,7 +11,6 @@
 LOG2E = 1.4426950408889634
 MESH = pl.DeviceIdType.MESH
 NEG = -1e30
-PAD = 16
 OUT = pltpu.VMEM
 
 
@@ -20,11 +19,12 @@
     q_hbm, k_hbm, v_hbm, len_hbm, win_hbm, w_hbm,
     o_1, o_2, judged_ref,
     q_v, k_o, v_o, k_x, v_x, q_x, k_s, k_c, v_s, v_c, vt, bias,
-    acc, top, len_ref, win_ref, w_ref, part_1, part_2, part_3, got_1, got_2, got_3,
+    acc, top, len_ref, win_ref, w_ref, part_1, part_2, got_1, got_2, got_3,
     load_sem, xs, xr, zs, zr, qs, qr, small_sem, ps, pr, z_in, core_in,
 ):
     half = span // 2
     ratio = heads // groups
+    pad = vt.shape[2] - HD
     me = lax.axis_index("cand")
     bit = lax.rem(me, 2)
     hd = lax.axis_index("head")
@@ -113,8 +113,26 @@
     tail = lax.broadcasted_iota(jnp.int32, (half, HD), 0) + half
     for i, n in enumerate((len_me, len_mate, len_s, len_c)):
         bias[i] = jnp.where(tail < n, 0.0, NEG).astype(jnp.float32)
-        for g in range(groups):
-            vt[i, g, HD:, :] = jnp.ones((PAD, span), jnp.bfloat16)
+
+    spare = lax.broadcasted_iota(jnp.int32, (pad, HD), 0)
+    scorer = []
+    for g in range(groups):
+        w = jnp.zeros((pad, HD), jnp.float32)
+        for j in range(ratio):
+            h = g * ratio + j
+            here = (spare == 1 + j) | (spare == 1 + ratio + j)
+            w = jnp.where(here, w_ref[h * HD : (h + 1) * HD].reshape(1, HD), w)
+        high = w.astype(jnp.bfloat16)
+        scorer.append((high, (w - high.astype(jnp.float32)).astype(jnp.bfloat16)))
+
+    def fill_vt(i, g, v):
+        t = jnp.transpose(v)
+        vt[i, g, :HD, :] = t
+        u = sum(jnp.dot(w, t, preferred_element_type=jnp.float32) for w in scorer[g])
+        high = u.astype(jnp.bfloat16).astype(jnp.float32)
+        row = lax.broadcasted_iota(jnp.int32, u.shape, 0)
+        u = jnp.where(row == 0, 1.0, jnp.where(row <= ratio, high, u - high))
+        vt[i, g, HD:, :] = u.astype(jnp.bfloat16)
 
     def scores(k, q):
         return lax.dot_general(k, q, (((1,), (1,)), ((), ())), preferred_element_type=jnp.float32)
@@ -133,14 +151,19 @@
         p = jnp.concatenate([jnp.exp2((s - peak) * scale).astype(jnp.bfloat16) for s in parts], axis=0)
         return jnp.dot(v, p, preferred_element_type=jnp.float32)
 
-    def finish(o, first_row, n):
-        rows = lax.broadcasted_iota(jnp.int32, (1, o.shape[1]), 1) + first_row
-        inverse = jnp.where(rows < n, 1.0 / o[HD : HD + 1], 0.0)
-        return jnp.transpose(o[:HD] * inverse).astype(jnp.bfloat16)
-
-    def judged(out, h):
-        x = jnp.sum(out.astype(jnp.float32).reshape(-1, 8, HD), axis=0)
-        return x * w_ref[h * HD : (h + 1) * HD].reshape(1, HD)
+    def inverse(total, first_row, n):
+        rows = lax.broadcasted_iota(jnp.int32, total.shape, 1) + first_row
+        return jnp.where(rows < n, 1.0 / total, 0.0)
+
+    def finish(o, scaled):
+        return jnp.transpose(o[:HD] * scaled).astype(jnp.bfloat16)
+
+    def judged(o, scaled, h):
+        row = lax.broadcasted_iota(jnp.int32, o.shape, 0)
+        j = h % ratio
+        x = jnp.where((row == 1 + j) | (row == 1 + ratio + j), o, 0.0) * scaled
+        x = sum(x[:, i : i + HD] for i in range(0, x.shape[1], HD))
+        return sum(x[i : i + 8] for i in range(0, pad, 8))
 
     def pipeline(items, first, rest):
         ahead = first(*items[0])
@@ -156,7 +179,7 @@
     for c in loads[: 2 * groups]:
         c.wait()
     for g in range(groups):
-        vt[0, g, :HD, :] = jnp.transpose(v_o[g])
+        fill_vt(0, g, v_o[g])
 
     def own_scores(h, c):
         if c == 0:
@@ -178,7 +201,7 @@
         x_copies[2 * g + 1].wait_recv()
         v_s[g] = jnp.where(i_won, v_o[g], v_x[g])
         f_copies[2 * g + 1].start()
-        vt[1, g, :HD, :] = jnp.transpose(v_x[g])
+        fill_vt(1, g, v_x[g])
 
     pipeline(group_blocks(0), own_scores, own_rest)
 
@@ -200,9 +223,9 @@
         peak = jnp.maximum(before, key_max(parts))
         keep = jnp.exp2((before - peak) * scale)
         o = weighted(parts, peak, vt[1, h // ratio]) + acc[h, :, c : c + half] * keep
-        out = finish(o, c, len_me)
-        o_1[h, c : c + half] = out
-        sums[1] += judged(out, h)
+        scaled = inverse(o[HD : HD + 1], c, len_me)
+        o_1[h, c : c + half] = finish(o, scaled)
+        sums[1] += judged(o[HD:], scaled, h)
 
     for g in range(groups):
         if g:
@@ -225,10 +248,10 @@
         a, b = masked(s[0], 2), masked(s[1], 3)
         peak = key_max(a + b)
         o = weighted(a, peak, vt[2, g]) + weighted(b, peak, vt[3, g])
-        out = finish(o, bit * half + r, len_s)
-        o_2[h, r : r + n] = out
+        scaled = inverse(o[HD : HD + 1], bit * half + r, len_s)
+        o_2[h, r : r + n] = finish(o, scaled)
         if h < early:
-            sums[2] += judged(out, h)
+            sums[2] += judged(o[HD:], scaled, h)
 
     def ahead_scores(h, c):
         return scores(k_c[h // ratio], q_v[h, c : c + half])
@@ -238,52 +261,47 @@
         before = top[h, :1, c : c + half]
         peak = jnp.maximum(before, key_max(parts))
         keep = jnp.exp2((before - peak) * scale)
-        o = weighted(parts, peak, vt[3, h // ratio]) + acc[h, :, c : c + half] * keep
-        sums[3] += judged(finish(o, c, len_me), h)
+        o = weighted(parts, peak, vt[3, h // ratio, HD:, :]) + acc[h, HD:, c : c + half] * keep
+        sums[3] += judged(o, inverse(o[:1], c, len_me), h)
 
     def over(x, n):
         return x / jnp.full((8, HD), n.astype(jnp.float32))
 
-    early = heads - ratio
     send_1 = remote(part_1, got_1, ps.at[0], pr.at[0], {"head": other})
     send_2 = remote(part_2, got_2, ps.at[1], pr.at[1], {"head": other})
-    send_3 = remote(part_3, got_3, ps.at[2], pr.at[2], {"cand": mate})
-
-    def challenger(g):
-        vt[2, g, :HD, :] = jnp.where(i_won, vt[0, g, :HD, :], vt[1, g, :HD, :])
-        for j in range(2):
-            f_copies[2 * g + j].wait_recv()
-        vt[3, g, :HD, :] = jnp.transpose(v_c[g])
+    send_3 = [
+        remote(x, got_3.at[i], ps.at[2 + i], pr.at[2 + i], {"cand": mate})
+        for i, x in enumerate((part_2, got_2))
+    ]
 
     def second(first, end):
         for i in range(first, end):
             second_rest(second_scores(i), i)
 
-    ahead = early // 2 + 1
-    challenger(0)
+    early = heads - ratio - 1
     send_1.start()
-    second(0, ahead)
-    for g in range(1, groups):
-        challenger(g)
-    pipeline(
-        [(h, c) for h in range(early, heads) for c in range(0, span, half)],
-        ahead_scores, ahead_rest,
-    )
-    second(ahead, early)
+    for g in range(groups):
+        vt[2, g] = jnp.where(i_won, vt[0, g], vt[1, g])
+        for j in range(2):
+            f_copies[2 * g + j].wait_recv()
+        fill_vt(3, g, v_c[g])
+        pipeline([b for b in group_blocks(g) if b[0] >= early], ahead_scores, ahead_rest)
+        if g == 0:
+            second(0, early)
     part_2[...] = sums[2] + jnp.where(i_won, sums[3], 0.0)
     send_1.wait()
     judged_ref[0] = over(part_1[...] + got_1[...], len_me)
     send_2.start()
-    second(early, early + 2)
-    send_2.wait()
-    part_3[...] = part_2[...] + got_2[...]
-    second(early + 2, early + 3)
-    send_3.start()
+    send_3[0].start()
+    second(early, early + 3)
+    send_2.wait_recv()
+    send_3[1].start()
     second(early + 3, len(chunks))
-    for c in x_copies + f_copies + q_copies:
+    for c in x_copies + f_copies + q_copies + [send_2]:
         c.wait_send()
-    send_3.wait()
-    judged_ref[1] = over(part_3[...] + got_3[...], len_s)
+    for c in send_3:
+        c.wait()
+    judged_ref[1] = over((part_2[...] + got_2[...]) + (got_3[0] + got_3[1]), len_s)
 
 
 def put_out(heads, o_1, o_2, judged_ref, first_hbm, second_hbm, s1_hbm, s2_hbm, s1, s2, sem):
@@ -312,6 +330,7 @@
     vmem = pl.BlockSpec(memory_space=pltpu.VMEM)
     dma = pltpu.SemaphoreType.DMA
     kv = pltpu.VMEM((groups, span, HD), bf16)
+    pad = pl.cdiv(1 + 2 * (heads // groups), 16) * 16
     o_1, o_2, judged = pl.pallas_call(
         functools.partial(kernel, heads, groups, span),
         out_shape=(
@@ -326,20 +345,21 @@
             kv, kv, kv, kv,
             pltpu.VMEM((heads, half, HD), bf16),
             kv, kv, kv, kv,
-            pltpu.VMEM((4, groups, HD + PAD, span), bf16),
+            pltpu.VMEM((4, groups, HD + pad, span), bf16),
             pltpu.VMEM((4, half, HD), f32),
-            pltpu.VMEM((heads, HD + PAD, span), f32),
+            pltpu.VMEM((heads, HD + pad, span), f32),
             pltpu.VMEM((heads, 8, span), f32),
             pltpu.SMEM(lengths.shape, jnp.int32),
             pltpu.SMEM(winners.shape, jnp.int32),
             pltpu.VMEM(score_weight.shape, f32),
-            *[pltpu.VMEM((8, HD), f32)] * 6,
+            *[pltpu.VMEM((8, HD), f32)] * 4,
+            pltpu.VMEM((2, 8, HD), f32),
             dma((2 * groups + heads,)),
             dma((2 * groups,)), dma((2 * groups,)),
             dma((2 * groups,)), dma((2 * groups,)),
             dma((heads + 1,)), dma((heads + 1,)),
             dma((3,)),
-            dma((3,)), dma((3,)),
+            dma((4,)), dma((4,)),
             pltpu.SemaphoreType.REGULAR((1,)), pltpu.SemaphoreType.REGULAR((1,)),
         ],
         compiler_params=pltpu.CompilerParams(collective_id=0, has_side_effects=True),

time: 34.6 us -> 33.9 us (0.980)
  Pallas kernels: 33.6 us -> 32.9 us
    pallas_call x1, Pallas kernels: 32.2 us -> 31.4 us  [body(): pl.pallas_call(functools.partial(kernel, heads, groups, span), out_shape=...]
where the time goes in v3:
time: 33.9 us; the launch traced here: 33.7 us
  Pallas kernels  32.9 us (97%)
  between operations  0.82 us (2%)
    pallas_call x1, Pallas kernels, body(): pl.pallas_call(functools.partial(kernel, heads, groups, span), out_shape=...  31.4 us
    pallas_call x1, Pallas kernels, body(): pl.pallas_call(functools.partial(put_out, heads), out_shape=(jax.ShapeDty...  1.46 us

profile of v3, /device:TPU:0, one launch (start us, length us, event | category | flops | bytes accessed | tf_op | source)
XLA Modules:
  0.0 33.7 jit_solution(11920091361583970579)
XLA Ops:
  0.6 31.4 %shard_map.93 = (bf16[10,512,128]{2,1,0:T(8,128)(2,1)S(1)}, bf16[10,256,128]{2,1,0:T(8,128)(2,1)S(1)}, f32[2,8,128]{2,1,0:T(8,128)S(1)}) custom-call(bf16[512,1280]{1,0:T(8,128)(2,1)} %q_hbm.1, bf16[512,256]{1,0:T(8,128)(2,1)} %k_hbm.1, bf16[512,256]{1,0:T(8,128)(2,1)} %v_hbm.1, s32[8]{0:T(128)} %len_hbm.1, s32[4]{0:T(128)} %win_hbm.1, f32[1280]{0:T(1024)} %w_hbm.1), custom_call_target="tpu_custom_call" | custom-call | tf_op jit(solution)/shard_map/pallas_call | solution.py:334
  32.1 1.5 %shard_map.94 = (bf16[512,1280]{1,0:T(8,128)(2,1)}, bf16[256,1280]{1,0:T(8,128)(2,1)}, f32[1]{0:T(128)}, f32[1]{0:T(128)}) custom-call(bf16[10,512,128]{2,1,0:T(8,128)(2,1)S(1)} %get-tuple-element.7.o_1, bf16[10,256,128]{2,1,0:T(8,128)(2,1)S(1)} %get-tuple-element.8.o_2, f32[2,8,128]{2,1,0:T(8,128)S(1)} %get-tuple-element.9.judged_ref), custom_call_target="tpu_custom_call" | custom-call | tf_op jit(solution)/shard_map/pallas_call | solution.py:367

commit v4 on v3

--- a/solution.py
+++ b/solution.py
@@ -19,7 +19,7 @@
     q_hbm, k_hbm, v_hbm, len_hbm, win_hbm, w_hbm,
     o_1, o_2, judged_ref,
     q_v, k_o, v_o, k_x, v_x, q_x, k_s, k_c, v_s, v_c, vt, bias,
-    acc, top, len_ref, win_ref, w_ref, part_1, part_2, got_1, got_2, got_3,
+    acc, top, len_ref, win_ref, w_ref, part_1, part_2, got_1, got_2,
     load_sem, xs, xr, zs, zr, qs, qr, small_sem, ps, pr, z_in, core_in,
 ):
     half = span // 2
@@ -76,12 +76,10 @@
             )
             f_copies.append(remote(fsrc.at[g], fdst.at[g], zs.at[i], zr.at[i], {"cand": across}))
 
-    quarter = half // 2
-    chunks = [(h, 0, half) for h in range(heads - 1)]
-    chunks += [(heads - 1, r, quarter) for r in (0, quarter)]
+    chunks = [(h, 0, half) for h in range(heads)]
     q_copies = []
     for i, (h, r, n) in enumerate(chunks):
-        rows = pl.ds(pl.multiple_of((1 - bit) * half + r, quarter), n)
+        rows = pl.ds(pl.multiple_of((1 - bit) * half + r, half), n)
         q_copies.append(
             remote(q_hbm.at[rows, col(h)], q_x.at[h, r : r + n], qs.at[i], qr.at[i], {"cand": mate})
         )
@@ -95,8 +93,10 @@
 
     @pl.when(hd == 1)
     def _():
-        pl.semaphore_signal(z_in.at[0], inc=1, device_id={"cand": across}, device_id_type=MESH)
-        pl.semaphore_wait(z_in.at[0], 1)
+        for i, peer in enumerate((across, mate)):
+            pl.semaphore_signal(z_in.at[i], inc=1, device_id={"cand": peer}, device_id_type=MESH)
+        for i in range(2):
+            pl.semaphore_wait(z_in.at[i], 1)
         pl.semaphore_signal(core_in.at[0], inc=1, device_id={"head": 0}, device_id_type=MESH)
 
     for c in small:
@@ -238,7 +238,7 @@
         h, r, n = chunks[i]
         g = h // ratio
         q_copies[i].wait_recv()
-        rows = pl.ds(pl.multiple_of(bit * half + r, quarter), n)
+        rows = pl.ds(pl.multiple_of(bit * half + r, half), n)
         q = jnp.where(i_won, q_v[h, rows, :], q_x[h, r : r + n])
         return scores(k_s[g], q), scores(k_c[g], q)
 
@@ -268,10 +268,9 @@
         return x / jnp.full((8, HD), n.astype(jnp.float32))
 
     send_1 = remote(part_1, got_1, ps.at[0], pr.at[0], {"head": other})
-    send_2 = remote(part_2, got_2, ps.at[1], pr.at[1], {"head": other})
-    send_3 = [
-        remote(x, got_3.at[i], ps.at[2 + i], pr.at[2 + i], {"cand": mate})
-        for i, x in enumerate((part_2, got_2))
+    send_2 = [
+        remote(part_2, got_2.at[i], ps.at[1 + i], pr.at[1 + i], peer)
+        for i, peer in enumerate(({"head": other}, {"cand": mate}, {"cand": mate, "head": other}))
     ]
 
     def second(first, end):
@@ -291,17 +290,14 @@
     part_2[...] = sums[2] + jnp.where(i_won, sums[3], 0.0)
     send_1.wait()
     judged_ref[0] = over(part_1[...] + got_1[...], len_me)
-    send_2.start()
-    send_3[0].start()
-    second(early, early + 3)
-    send_2.wait_recv()
-    send_3[1].start()
-    second(early + 3, len(chunks))
-    for c in x_copies + f_copies + q_copies + [send_2]:
+    for c in send_2:
+        c.start()
+    second(early, len(chunks))
+    for c in x_copies + f_copies + q_copies:
         c.wait_send()
-    for c in send_3:
+    for c in send_2:
         c.wait()
-    judged_ref[1] = over((part_2[...] + got_2[...]) + (got_3[0] + got_3[1]), len_s)
+    judged_ref[1] = over((part_2[...] + got_2[0]) + (got_2[1] + got_2[2]), len_s)
 
 
 def put_out(heads, o_1, o_2, judged_ref, first_hbm, second_hbm, s1_hbm, s2_hbm, s1, s2, sem):
@@ -352,15 +348,15 @@
             pltpu.SMEM(lengths.shape, jnp.int32),
             pltpu.SMEM(winners.shape, jnp.int32),
             pltpu.VMEM(score_weight.shape, f32),
-            *[pltpu.VMEM((8, HD), f32)] * 4,
-            pltpu.VMEM((2, 8, HD), f32),
+            *[pltpu.VMEM((8, HD), f32)] * 3,
+            pltpu.VMEM((3, 8, HD), f32),
             dma((2 * groups + heads,)),
             dma((2 * groups,)), dma((2 * groups,)),
             dma((2 * groups,)), dma((2 * groups,)),
-            dma((heads + 1,)), dma((heads + 1,)),
+            dma((heads,)), dma((heads,)),
             dma((3,)),
             dma((4,)), dma((4,)),
-            pltpu.SemaphoreType.REGULAR((1,)), pltpu.SemaphoreType.REGULAR((1,)),
+            pltpu.SemaphoreType.REGULAR((2,)), pltpu.SemaphoreType.REGULAR((1,)),
         ],
         compiler_params=pltpu.CompilerParams(collective_id=0, has_side_effects=True),
     )(queries, keys, values, lengths, winners, score_weight)

time: 33.9 us -> 33.4 us (0.985)
  Pallas kernels: 32.9 us -> 32.5 us
    pallas_call x1, Pallas kernels: 31.4 us -> 31 us  [body(): pl.pallas_call(functools.partial(kernel, heads, groups, span), out_shape=...]
where the time goes in v4:
time: 33.4 us; the launch traced here: 33.3 us
  Pallas kernels  32.5 us (97%)
  between operations  0.8 us (2%)
    pallas_call x1, Pallas kernels, body(): pl.pallas_call(functools.partial(kernel, heads, groups, span), out_shape=...  31 us
    pallas_call x1, Pallas kernels, body(): pl.pallas_call(functools.partial(put_out, heads), out_shape=(jax.ShapeDty...  1.46 us

profile of v4, /device:TPU:0, one launch (start us, length us, event | category | flops | bytes accessed | tf_op | source)
XLA Modules:
  0.0 33.3 jit_solution(17540542871871304592)
XLA Ops:
  0.6 31.0 %shard_map.93 = (bf16[10,512,128]{2,1,0:T(8,128)(2,1)S(1)}, bf16[10,256,128]{2,1,0:T(8,128)(2,1)S(1)}, f32[2,8,128]{2,1,0:T(8,128)S(1)}) custom-call(bf16[512,1280]{1,0:T(8,128)(2,1)} %q_hbm.1, bf16[512,256]{1,0:T(8,128)(2,1)} %k_hbm.1, bf16[512,256]{1,0:T(8,128)(2,1)} %v_hbm.1, s32[8]{0:T(128)} %len_hbm.1, s32[4]{0:T(128)} %win_hbm.1, f32[1280]{0:T(1024)} %w_hbm.1), custom_call_target="tpu_custom_call" | custom-call | tf_op jit(solution)/shard_map/pallas_call | solution.py:330
  31.7 1.5 %shard_map.94 = (bf16[512,1280]{1,0:T(8,128)(2,1)}, bf16[256,1280]{1,0:T(8,128)(2,1)}, f32[1]{0:T(128)}, f32[1]{0:T(128)}) custom-call(bf16[10,512,128]{2,1,0:T(8,128)(2,1)S(1)} %get-tuple-element.7.o_1, bf16[10,256,128]{2,1,0:T(8,128)(2,1)S(1)} %get-tuple-element.8.o_2, f32[2,8,128]{2,1,0:T(8,128)S(1)} %get-tuple-element.9.judged_ref), custom_call_target="tpu_custom_call" | custom-call | tf_op jit(solution)/shard_map/pallas_call | solution.py:363

commit v5 on v4

--- a/solution.py
+++ b/solution.py
@@ -19,7 +19,7 @@
     q_hbm, k_hbm, v_hbm, len_hbm, win_hbm, w_hbm,
     o_1, o_2, judged_ref,
     q_v, k_o, v_o, k_x, v_x, q_x, k_s, k_c, v_s, v_c, vt, bias,
-    acc, top, len_ref, win_ref, w_ref, part_1, part_2, got_1, got_2,
+    acc, top, o_r, len_ref, win_ref, w_ref, part_1, part_2, got_1, got_2,
     load_sem, xs, xr, zs, zr, qs, qr, small_sem, ps, pr, z_in, core_in,
 ):
     half = span // 2
@@ -76,20 +76,25 @@
             )
             f_copies.append(remote(fsrc.at[g], fdst.at[g], zs.at[i], zr.at[i], {"cand": across}))
 
-    chunks = [(h, 0, half) for h in range(heads)]
-    q_copies = []
-    for i, (h, r, n) in enumerate(chunks):
-        rows = pl.ds(pl.multiple_of((1 - bit) * half + r, half), n)
-        q_copies.append(
-            remote(q_hbm.at[rows, col(h)], q_x.at[h, r : r + n], qs.at[i], qr.at[i], {"cand": mate})
+    made = list(range(ratio - 2, ratio))
+    asked = [h for h in range(heads) if h not in made]
+    late = asked[-3:]
+    sent = pl.ds(pl.multiple_of((1 - bit) * half, half), half)
+    mine = pl.ds(pl.multiple_of(bit * half, half), half)
+    q_copies = {
+        h: remote(
+            o_r.at[made.index(h), sent] if h in made else q_hbm.at[sent, col(h)],
+            q_x.at[h], qs.at[h], qr.at[h], {"cand": mate},
         )
+        for h in range(heads)
+    }
 
     for c in x_copies:
         c.start()
     for c in small + loads:
         c.start()
-    for c in q_copies:
-        c.start()
+    for h in asked:
+        q_copies[h].start()
 
     @pl.when(hd == 1)
     def _():
@@ -234,23 +239,16 @@
         pipeline(group_blocks(g), mate_scores, mate_rest)
     part_1[...] = sums[1]
 
-    def second_scores(i):
-        h, r, n = chunks[i]
+    def second(h):
         g = h // ratio
-        q_copies[i].wait_recv()
-        rows = pl.ds(pl.multiple_of(bit * half + r, half), n)
-        q = jnp.where(i_won, q_v[h, rows, :], q_x[h, r : r + n])
-        return scores(k_s[g], q), scores(k_c[g], q)
-
-    def second_rest(s, i):
-        h, r, n = chunks[i]
-        g = h // ratio
-        a, b = masked(s[0], 2), masked(s[1], 3)
+        q_copies[h].wait_recv()
+        q = jnp.where(i_won, q_v[h, mine, :], q_x[h])
+        a, b = masked(scores(k_s[g], q), 2), masked(scores(k_c[g], q), 3)
         peak = key_max(a + b)
         o = weighted(a, peak, vt[2, g]) + weighted(b, peak, vt[3, g])
-        scaled = inverse(o[HD : HD + 1], bit * half + r, len_s)
-        o_2[h, r : r + n] = finish(o, scaled)
-        if h < early:
+        scaled = inverse(o[HD : HD + 1], bit * half, len_s)
+        o_2[h] = finish(o, scaled)
+        if h not in late:
             sums[2] += judged(o[HD:], scaled, h)
 
     def ahead_scores(h, c):
@@ -261,8 +259,16 @@
         before = top[h, :1, c : c + half]
         peak = jnp.maximum(before, key_max(parts))
         keep = jnp.exp2((before - peak) * scale)
-        o = weighted(parts, peak, vt[3, h // ratio, HD:, :]) + acc[h, HD:, c : c + half] * keep
-        sums[3] += judged(o, inverse(o[:1], c, len_me), h)
+        skip = 0 if h in made else HD
+        o = weighted(parts, peak, vt[3, h // ratio, skip:, :])
+        o += acc[h, skip:, c : c + half] * keep
+        scaled = inverse(o[HD - skip : HD - skip + 1], c, len_me)
+        if h in made:
+            o_r[made.index(h), c : c + half] = finish(o, scaled)
+        sums[3] += judged(o[HD - skip :], scaled, h)
+
+    def ahead(some):
+        pipeline([(h, c) for h in some for c in range(0, span, half)], ahead_scores, ahead_rest)
 
     def over(x, n):
         return x / jnp.full((8, HD), n.astype(jnp.float32))
@@ -273,27 +279,36 @@
         for i, peer in enumerate(({"head": other}, {"cand": mate}, {"cand": mate, "head": other}))
     ]
 
-    def second(first, end):
-        for i in range(first, end):
-            second_rest(second_scores(i), i)
-
-    early = heads - ratio - 1
-    send_1.start()
-    for g in range(groups):
+    def challenger(g):
         vt[2, g] = jnp.where(i_won, vt[0, g], vt[1, g])
         for j in range(2):
             f_copies[2 * g + j].wait_recv()
         fill_vt(3, g, v_c[g])
-        pipeline([b for b in group_blocks(g) if b[0] >= early], ahead_scores, ahead_rest)
-        if g == 0:
-            second(0, early)
+
+    send_1.start()
+    challenger(0)
+    ahead(made)
+    second(asked[0])
+    for h in made:
+        q_copies[h].start()
+    for h in asked[1 : ratio - 2]:
+        second(h)
+    for g in range(1, groups):
+        challenger(g)
+    for h in asked[ratio - 2 : -3]:
+        second(h)
+    ahead(late)
     part_2[...] = sums[2] + jnp.where(i_won, sums[3], 0.0)
     send_1.wait()
     judged_ref[0] = over(part_1[...] + got_1[...], len_me)
     for c in send_2:
         c.start()
-    second(early, len(chunks))
-    for c in x_copies + f_copies + q_copies:
+    for h in late:
+        second(h)
+    for i, h in enumerate(made):
+        q_copies[h].wait_recv()
+        o_2[h] = jnp.where(i_won, o_r[i, mine, :], q_x[h])
+    for c in x_copies + f_copies + list(q_copies.values()):
         c.wait_send()
     for c in send_2:
         c.wait()
@@ -345,6 +360,7 @@
             pltpu.VMEM((4, half, HD), f32),
             pltpu.VMEM((heads, HD + pad, span), f32),
             pltpu.VMEM((heads, 8, span), f32),
+            pltpu.VMEM((2, span, HD), bf16),
             pltpu.SMEM(lengths.shape, jnp.int32),
             pltpu.SMEM(winners.shape, jnp.int32),
             pltpu.VMEM(score_weight.shape, f32),

time: 33.4 us -> 33.2 us (level)
  no operation moved by 1% of the time
where the time goes in v5:
time: 33.2 us; the launch traced here: 33.1 us
  Pallas kernels  32.3 us (97%)
  between operations  0.8 us (2%)
    pallas_call x1, Pallas kernels, body(): pl.pallas_call(functools.partial(kernel, heads, groups, span), out_shape=...  30.8 us
    pallas_call x1, Pallas kernels, body(): pl.pallas_call(functools.partial(put_out, heads), out_shape=(jax.ShapeDty...  1.46 us

profile of v5, /device:TPU:0, one launch (start us, length us, event | category | flops | bytes accessed | tf_op | source)
XLA Modules:
  0.0 33.1 jit_solution(5722962215411117131)
XLA Ops:
  0.6 30.8 %shard_map.93 = (bf16[10,512,128]{2,1,0:T(8,128)(2,1)S(1)}, bf16[10,256,128]{2,1,0:T(8,128)(2,1)S(1)}, f32[2,8,128]{2,1,0:T(8,128)S(1)}) custom-call(bf16[512,1280]{1,0:T(8,128)(2,1)} %q_hbm.1, bf16[512,256]{1,0:T(8,128)(2,1)} %k_hbm.1, bf16[512,256]{1,0:T(8,128)(2,1)} %v_hbm.1, s32[8]{0:T(128)} %len_hbm.1, s32[4]{0:T(128)} %win_hbm.1, f32[1280]{0:T(1024)} %w_hbm.1), custom_call_target="tpu_custom_call" | custom-call | tf_op jit(solution)/shard_map/pallas_call | solution.py:345
  31.5 1.5 %shard_map.94 = (bf16[512,1280]{1,0:T(8,128)(2,1)}, bf16[256,1280]{1,0:T(8,128)(2,1)}, f32[1]{0:T(128)}, f32[1]{0:T(128)}) custom-call(bf16[10,512,128]{2,1,0:T(8,128)(2,1)S(1)} %get-tuple-element.7.o_1, bf16[10,256,128]{2,1,0:T(8,128)(2,1)S(1)} %get-tuple-element.8.o_2, f32[2,8,128]{2,1,0:T(8,128)S(1)} %get-tuple-element.9.judged_ref), custom_call_target="tpu_custom_call" | custom-call | tf_op jit(solution)/shard_map/pallas_call | solution.py:379

commit v6 on v5

--- a/solution.py
+++ b/solution.py
@@ -289,20 +289,22 @@
     challenger(0)
     ahead(made)
     second(asked[0])
-    for h in made:
+    for h in made[:-1]:
         q_copies[h].start()
     for h in asked[1 : ratio - 2]:
         second(h)
     for g in range(1, groups):
         challenger(g)
-    for h in asked[ratio - 2 : -3]:
+    second(asked[ratio - 2])
+    ahead(late)
+    for h in asked[ratio - 1 : -3]:
         second(h)
-    ahead(late)
     part_2[...] = sums[2] + jnp.where(i_won, sums[3], 0.0)
     send_1.wait()
     judged_ref[0] = over(part_1[...] + got_1[...], len_me)
     for c in send_2:
         c.start()
+    q_copies[made[-1]].start()
     for h in late:
         second(h)
     for i, h in enumerate(made):

time: 33.2 us -> 33.1 us (level)
  no operation moved by 1% of the time
where the time goes in v6:
time: 33.1 us; the launch traced here: 32.9 us
  Pallas kernels  32.1 us (97%)
  between operations  0.8 us (2%)
    pallas_call x1, Pallas kernels, body(): pl.pallas_call(functools.partial(kernel, heads, groups, span), out_shape=...  30.6 us
    pallas_call x1, Pallas kernels, body(): pl.pallas_call(functools.partial(put_out, heads), out_shape=(jax.ShapeDty...  1.46 us

profile of v6, /device:TPU:0, one launch (start us, length us, event | category | flops | bytes accessed | tf_op | source)
XLA Modules:
  0.0 32.9 jit_solution(11599335299262642434)
XLA Ops:
  0.6 30.6 %shard_map.93 = (bf16[10,512,128]{2,1,0:T(8,128)(2,1)S(1)}, bf16[10,256,128]{2,1,0:T(8,128)(2,1)S(1)}, f32[2,8,128]{2,1,0:T(8,128)S(1)}) custom-call(bf16[512,1280]{1,0:T(8,128)(2,1)} %q_hbm.1, bf16[512,256]{1,0:T(8,128)(2,1)} %k_hbm.1, bf16[512,256]{1,0:T(8,128)(2,1)} %v_hbm.1, s32[8]{0:T(128)} %len_hbm.1, s32[4]{0:T(128)} %win_hbm.1, f32[1280]{0:T(1024)} %w_hbm.1), custom_call_target="tpu_custom_call" | custom-call | tf_op jit(solution)/shard_map/pallas_call | solution.py:347
  31.3 1.5 %shard_map.94 = (bf16[512,1280]{1,0:T(8,128)(2,1)}, bf16[256,1280]{1,0:T(8,128)(2,1)}, f32[1]{0:T(128)}, f32[1]{0:T(128)}) custom-call(bf16[10,512,128]{2,1,0:T(8,128)(2,1)S(1)} %get-tuple-element.7.o_1, bf16[10,256,128]{2,1,0:T(8,128)(2,1)S(1)} %get-tuple-element.8.o_2, f32[2,8,128]{2,1,0:T(8,128)S(1)} %get-tuple-element.9.judged_ref), custom_call_target="tpu_custom_call" | custom-call | tf_op jit(solution)/shard_map/pallas_call | solution.py:381
